TPU v7x, 256 devices: a whole 4x4x8 slice. The times are simulated.
256 devices in a mesh: ctx: 64 (over z, x, core), head: 4 (over y).
Axes of the slice: x: 4, y: 4, z: 8, core: 2. Of those that a mesh axis runs over, the one named last changes fastest.
Arguments:
- queries: bfloat16 [65536, 1024], P('ctx', 'head'), may hold values from -6 to 6
- keys: bfloat16 [65536, 1024], P('ctx', 'head'), may hold values from -6 to 6
- values: bfloat16 [65536, 1024], P('ctx', 'head'), may hold values from -6 to 6
- level_index: int32 [65536], P('ctx'), may hold values from 0 to 15
- level_table: float32 [16, 8, 11], P(None, 'head'), may hold values from 0.2 to 2
- head_gain: float32 [1024], P('head'), may hold values from 0.5 to 1.5
- residual: bfloat16 [65536, 1024], P(('ctx', 'head')), may hold values from -6 to 6
- w_out: bfloat16 [1024, 1024], replicated, may hold values from -0.1875 to 0.1875
- norm_gain: float32 [1024], replicated, may hold values from 0.5 to 1.5
- w_qkv: bfloat16 [1024, 3072], replicated, may hold values from -8 to 8
- windows: int32 [8], replicated, may hold values from 64 to 256, as said below
Outputs:
- hidden: bfloat16 [65536, 1024], P(('ctx', 'head'))
- attended: bfloat16 [65536, 1024], P('ctx', 'head')
Inputs may be any that keep to these rules, and one draw needn't show every extreme that they name: `windows`: each head's key window; some head's window is exactly 256 in every draw.
All inputs are finite; a program needn't handle non-finite values.
Results may differ from a plain program's by a relative error of at most 0.014.
Values may be sent and summed in bfloat16 or wider, within the bound.
No kernel may reach another device: no remote copies, remote signals or barrier semaphores. Data moves between devices by JAX's collectives and lax.ppermute only.
A program may use at most 128 MiB of HBM per device.

v0:
```python
import jax
import jax.numpy as jnp
from jax import lax
from jax.sharding import PartitionSpec as P

STRETCH = 64
WINDOW = 256
EPSILON = 1e-05
PRECISE = lax.Precision.HIGHEST


def from_behind(block, axis, distance):
    devices = range(lax.axis_size(axis))
    route = [(i - distance, i) for i in devices if i - distance in devices]
    return lax.ppermute(block, axis, route)


def bfloat(array):
    return array.astype(jnp.bfloat16)


def attend_block(
    query_block, key_block, value_block, head_windows, query_pos, key_pos, score_scale
):
    scores = (
        jnp.einsum("qhd,khd->hqk", query_block, key_block, preferred_element_type=jnp.float32)
        * score_scale
    )
    distance = query_pos[:, None] - key_pos[None, :]
    allowed = (
        (distance >= 0)[None]
        & (distance < head_windows[:, None, None])
        & (key_pos >= 0)[None, None, :]
    )
    scores = jnp.where(allowed, scores, -1e30)
    row_max = jnp.max(scores, -1, keepdims=True)
    weights = jnp.exp(scores - row_max)
    probs = bfloat(weights / jnp.sum(weights, -1, keepdims=True))
    return bfloat(
        jnp.einsum("hqk,khd->qhd", probs, value_block, preferred_element_type=jnp.float32)
    )


def windowed(query_rows, key_value, head_windows, first_pos, context_rows, score_scale):
    query_count = query_rows.shape[0]
    block_rows = min(query_count, 512)
    block_count = query_count // block_rows

    def attend_one(block_index):
        offset = block_index * block_rows
        query_block = lax.dynamic_slice_in_dim(query_rows, offset, block_rows, 0)
        pair_block = lax.dynamic_slice_in_dim(key_value, offset, context_rows + block_rows, 0)
        query_pos = first_pos + offset + jnp.arange(block_rows, dtype=jnp.int32)
        key_pos = (
            first_pos
            + offset
            - context_rows
            + jnp.arange(context_rows + block_rows, dtype=jnp.int32)
        )
        return attend_block(
            query_block,
            pair_block[:, 0],
            pair_block[:, 1],
            head_windows,
            query_pos,
            key_pos,
            score_scale,
        )

    results = lax.map(attend_one, jnp.arange(block_count, dtype=jnp.int32))
    return results.reshape((query_count,) + query_rows.shape[1:])


def per_device(
    queries,
    keys,
    values,
    level_index,
    level_table,
    head_gain,
    residual,
    w_out,
    norm_gain,
    w_qkv,
    windows,
):
    token_count = queries.shape[0]
    local_heads = level_table.shape[1]
    levels = level_table.shape[2]
    head_dim = head_gain.shape[0] // local_heads
    stretch_len = STRETCH
    stretches = token_count // stretch_len
    local_bits = stretches.bit_length() - 1
    ctx_bits = lax.axis_size("ctx").bit_length() - 1
    position = lax.axis_index("ctx")
    stretch_shape = (stretches, stretch_len, local_heads, head_dim)
    query_stretches = queries.reshape(stretch_shape)
    key_stretches = keys.reshape(stretch_shape)
    value_stretches = values.reshape(stretch_shape)
    states = jnp.einsum(
        "jchd,jche->jhde", key_stretches, value_stretches, preferred_element_type=jnp.float32
    )
    device_state = jnp.sum(states, 0).reshape(local_heads * head_dim, head_dim)
    piece = lax.all_gather(device_state[None], "ctx", axis=0, tiled=True)
    piece_rows = piece.shape[0]
    source = jnp.arange(piece_rows, dtype=jnp.int32)
    span_sizes = 2 ** jnp.arange(ctx_bits, dtype=jnp.int32)
    lower_edge = position // (2 * span_sizes) * (2 * span_sizes)
    upper_edge = position // span_sizes * span_sizes
    member = ((source[:, None] >= lower_edge[None]) & (source[:, None] < upper_edge[None])).astype(
        jnp.float32
    )
    remote = jnp.einsum("nb,nxy->bxy", member, piece, precision=PRECISE)
    level_rows = level_table.reshape(level_table.shape[0], local_heads * levels)
    onehot = (
        level_index[:, None] == jnp.arange(level_rows.shape[0], dtype=jnp.int32)[None]
    ).astype(jnp.float32)
    level_weight = jnp.dot(onehot, level_rows, precision=PRECISE).reshape(
        stretches, stretch_len, local_heads, levels
    )
    causal = (
        jnp.arange(stretch_len, dtype=jnp.int32)[:, None]
        >= jnp.arange(stretch_len, dtype=jnp.int32)[None, :]
    )
    scores = jnp.einsum(
        "jthd,jshd->jhts", query_stretches, key_stretches, preferred_element_type=jnp.float32
    )
    scores = bfloat(jnp.where(causal[None, None], scores, 0.0))
    inside = jnp.einsum(
        "jhts,jshd->jthd", scores, value_stretches, preferred_element_type=jnp.float32
    )
    running = level_weight[..., 0:1] * stretch_len ** (-0.5) * inside
    for level_bit in range(local_bits):
        block_len = 2**level_bit
        group_total = stretches // block_len
        grouped = jnp.sum(
            states.reshape(group_total, block_len, local_heads, head_dim, head_dim), 1
        )
        earlier = jnp.concatenate([jnp.zeros_like(grouped[:1]), grouped[:-1]], 0)
        odd_mask = (jnp.arange(group_total, dtype=jnp.int32) % 2).astype(jnp.float32)
        read_state = bfloat(earlier * odd_mask[:, None, None, None])
        blocked_query = query_stretches.reshape(
            group_total, block_len * stretch_len, local_heads, head_dim
        )
        part_sum = jnp.einsum(
            "mthd,mhde->mthe", blocked_query, read_state, preferred_element_type=jnp.float32
        )
        weight_now = level_weight[..., 1 + level_bit : 2 + level_bit] * (
            stretch_len * block_len
        ) ** (-0.5)
        running = running + weight_now * part_sum.reshape(stretch_shape)
    remote_read = bfloat(remote.reshape(ctx_bits, local_heads, head_dim, head_dim))
    flat_query = queries.reshape(token_count, local_heads, head_dim)
    far_terms = jnp.einsum(
        "thd,bhde->tbhe", flat_query, remote_read, preferred_element_type=jnp.float32
    )
    far_rates = jnp.array(
        [(stretch_len * 2 ** (local_bits + level_bit)) ** (-0.5) for level_bit in range(ctx_bits)],
        jnp.float32,
    )
    far_weights = (
        level_weight.reshape(token_count, local_heads, levels)[:, :, 1 + local_bits :] * far_rates
    )
    running = running.reshape(token_count, local_heads, head_dim) + jnp.einsum(
        "tbhe,thb->the", far_terms, far_weights, precision=PRECISE
    )
    mean_square = jnp.mean(running * running, -1, keepdims=True)
    heads_out = bfloat(
        running * lax.rsqrt(mean_square + EPSILON) * head_gain.reshape(local_heads, head_dim)
    )
    group_count = lax.axis_size("head")
    row_count = token_count // group_count
    sectioned = heads_out.reshape(group_count, row_count, local_heads * head_dim)
    projected = jnp.einsum(
        "grc,cd->grd",
        lax.all_to_all(sectioned, "head", split_axis=0, concat_axis=2, tiled=True),
        w_out,
        preferred_element_type=jnp.float32,
    )
    hidden = bfloat(residual.astype(jnp.float32) + projected[0])
    hidden_f = hidden.astype(jnp.float32)
    normed = bfloat(
        hidden_f * lax.rsqrt(jnp.mean(hidden_f * hidden_f, -1, keepdims=True) + EPSILON) * norm_gain
    )
    projected_qkv = bfloat(jnp.dot(normed, w_qkv, preferred_element_type=jnp.float32))
    score_scale = head_dim ** (-0.5)
    split_qkv = projected_qkv.reshape(row_count, 3, group_count, local_heads * head_dim)
    local_qkv = lax.all_to_all(split_qkv, "head", split_axis=2, concat_axis=0, tiled=True)
    local_qkv = local_qkv.reshape(token_count, 3, local_heads, head_dim)
    tail_len = min(token_count, WINDOW)
    need_count = (WINDOW - 1 + token_count - 1) // token_count
    tail_pairs = local_qkv[token_count - tail_len :, 1:3]
    before = [from_behind(tail_pairs, "ctx", 1)]
    key_value = jnp.concatenate(before + [local_qkv[:, 1:3]], 0)
    head_windows = lax.dynamic_slice_in_dim(
        windows, lax.axis_index("head") * local_heads, local_heads
    )
    first_pos = position * token_count
    result = windowed(
        local_qkv[:, 0], key_value, head_windows, first_pos, need_count * tail_len, score_scale
    )
    return (hidden, result.reshape(token_count, local_heads * head_dim))


def solution(mesh):
    in_specs = (
        P("ctx", "head"),
        P("ctx", "head"),
        P("ctx", "head"),
        P("ctx"),
        P(None, "head", None),
        P("head"),
        P(("ctx", "head"), None),
        P(),
        P(),
        P(),
        P(),
    )
    out_specs = (P(("ctx", "head"), None), P("ctx", "head"))
    return jax.shard_map(
        per_device, mesh=mesh, in_specs=in_specs, out_specs=out_specs, check_vma=False
    )
```

profile of v0, /device:TPU:32, one launch (start us, length us, event | category | flops | bytes accessed | tf_op | source)
XLA Modules:
  0.0 231.0 jit_solution(5243764467069019587)
XLA Ops:
  8.5 2.0 reshape.270
  10.6 3.6 %fusion.96 = (f32[2,128,128]{2,1,0:T(8,128)}, f32[16,2,128,128]{3,2,1,0:T(8,128)}) fusion(bf16[16,64,2,128]{3,2,1,0:T(2,128)(2,1)} %reshape.270, bf16[16,64,2,128]{3,2,1,0:T(2,128)(2,1)S(1)} %reshape.269), kind=kOutput, calls=%fused_computation.147 | convolution fusion | flops 67600384 | bytes 3276800 | tf_op jit(solution)/shard_map/jchd,jche->jhde/dot_general | solution.py:100
  19.6 3.2 %slice.68 = f32[15,2,128,128]{3,2,1,0:T(8,128)} slice(f32[16,2,128,128]{3,2,1,0:T(8,128)} %get-tuple-element.135), slice={[0:15], [0:2], [0:128], [0:128]} | slice | bytes 3932160 | tf_op jit(solution)/shard_map/slice | solution.py:139
  27.8 2.6 %copy.101 = f32[4,256,2,128]{3,1,0,2:T(8,128)} copy(f32[4,256,2,128]{1,3,2,0:T(8,128)} %convolution_bitcast_fusion.2) | data formatting | bytes 2097152 | tf_op jit(solution)/shard_map/mthd,mhde->mthe/transpose | solution.py:145
  30.4 1.7 bitcast_reduce_fusion
  33.6 2.6 %copy.106 = f32[2,512,2,128]{3,1,0,2:T(8,128)} copy(f32[2,512,2,128]{1,3,2,0:T(8,128)} %convolution_bitcast_fusion.1) | data formatting | bytes 2097152 | tf_op jit(solution)/shard_map/mthd,mhde->mthe/transpose | solution.py:145
  36.3 3.2 %fusion.36 = f32[16,64,2,128]{3,1,2,0:T(8,128)} fusion(f32[15,2,128,128]{3,2,1,0:T(8,128)} %slice.68, f32[16]{0:T(128)S(1)} %fusion.84, f32[16,64,2]{1,2,0:T(2,128)S(1)} %copy.90, bf16[16,64,2,128]{3,2,1,0:T(2,128)(2,1)} %reshape.268), kind=kOutput, calls=%fused_computation.54 | convolution fusion | flops 68419584 | bytes 3547200 | tf_op jit(solution)/shard_map/mthd,mhde->mthe/dot_general | solution.py:145
  39.5 4.6 %fusion.35 = f32[16,64,2,128]{3,1,2,0:T(8,128)} fusion(f32[16,64,2,128]{3,1,2,0:T(8,128)} %fusion.36, f32[16,64,2,128]{3,1,0,2:T(8,128)} %bitcast.120, f32[16,64,2,128]{3,1,0,2:T(8,128)} %bitcast.119, f32[16,64,2,128]{3,1,0,2:T(8,128)} %bitcast.118, f32[16,64,2]{1,2,0:T(2,128)S(1)} %copy.103, f32[16,64,2]{1,2,0:T(2,128)S(1)} %copy.98, ...), kind=kOutput, calls=%fused_computation.52 | convolution fusion | flops 69468160 | bytes 6852608 | tf_op jit(solution)/shard_map/jhts,jshd->jthd/dot_general | solution.py:129
  45.7 53.9 %all-gather.2.cloned.1.call-done = f32[64,256,128]{2,1,0:T(8,128)} async-done(((f32[1,256,128]{2,1,0:T(8,128)}), f32[64,256,128]{2,1,0:T(8,128)}) %all-gather.2.cloned.1.call-update) | async-done | bytes 8388624 | tf_op jit(solution)/shard_map/all_gather | solution.py:104
  99.5 10.7 %fusion.39 = bf16[6,256,128]{2,0,1:T(8,128)(2,1)S(1)} fusion(f32[64,256,128]{2,1,0:T(8,128)} %all-gather.2.cloned.1.call-done, s32[6]{0:T(128)S(1)} %get-tuple-element.138, s32[6]{0:T(128)S(1)} %get-tuple-element.139), kind=kOutput, calls=%fused_computation.61 | convolution fusion | flops 151192704 | bytes 8781872 | tf_op jit(solution)/shard_map/nb,nxy->bxy/dot_general | solution.py:113
  110.2 2.0 fusion.30
  112.2 2.6 %copy.129 = f32[1024,2,128]{2,0,1:T(8,128)} copy(f32[1024,2,128]{0,2,1:T(8,128)} %fusion.30) | data formatting | bytes 2097152 | tf_op jit(solution)/shard_map/tbhe,thb->the/dot_general | solution.py:164
  114.9 1.7 multiply_reduce_fusion
  117.9 14.0 %all_to_all.30 = bf16[4,256,256]{2,1,0:T(8,128)(2,1)S(1)} all-to-all(bf16[4,256,256]{2,1,0:T(8,128)(2,1)S(1)} %reshape.279), channel_id=1, replica_groups=mesh['ctx'=64,'head'=4] {'head'}, dimensions={0} | all-to-all | bytes 1048576 | tf_op jit(solution)/shard_map/all_to_all | solution.py:176
  132.0 1.9 fusion.42
  134.7 5.8 %convolution_convert_fusion = bf16[256,3072]{1,0:T(8,128)(2,1)} fusion(bf16[1024,3072]{1,0:T(8,128)(2,1)} %param.23, bf16[256,1024]{1,0:T(8,128)(2,1)S(1)} %get-tuple-element.137, f32[1024]{0:T(1024)S(1)} %copy-done.15, f32[256]{0:T(256)S(1)} %add_rsqrt_fusion.1), kind=kOutput, calls=%fused_computation.38 | convolution fusion | flops 1612447744 | bytes 8393728 | tf_op jit(solution)/shard_map/dot_general | solution.py:185
  140.6 4.2 %reshape.281 = bf16[256,3,4,256]{3,2,1,0:T(4,128)(2,1)} reshape(bf16[256,3072]{1,0:T(8,128)(2,1)} %convolution_convert_fusion) | data formatting | bytes 3145728 | tf_op jit(solution)/shard_map/reshape | solution.py:187
  144.8 1.6 copy.114
  146.4 22.7 %all_to_all.31 = bf16[256,3,4,256]{3,0,1,2:T(8,128)(2,1)S(1)} all-to-all(bf16[256,3,4,256]{3,0,1,2:T(8,128)(2,1)S(1)} %copy.114), channel_id=1, replica_groups=mesh['ctx'=64,'head'=4] {'head'}, dimensions={2} | all-to-all | bytes 3145728 | tf_op jit(solution)/shard_map/all_to_all | solution.py:188
  170.4 3.5 %reshape.282 = bf16[1024,3,2,128]{3,2,0,1:T(2,128)(2,1)} reshape(bf16[4,256,3,1,256]{4,1,0,2,3:T(8,128)(2,1)} %copy.115) | data formatting | bytes 3145728 | tf_op jit(solution)/shard_map/reshape | solution.py:189
  173.9 1.9 slice.76
  175.8 2.1 collective-permute-start
  180.6 5.3 %collective-permute-done = bf16[256,2,2,128]{3,2,0,1:T(2,128)(2,1)S(1)} collective-permute-done((bf16[256,2,2,128]{3,2,0,1:T(2,128)(2,1)}, bf16[256,2,2,128]{3,2,0,1:T(2,128)(2,1)S(1)}, u32[]{:S(2)}, u32[]{:S(2)}) %collective-permute-start) | collective-permute-done | bytes 262176 | tf_op jit(solution)/shard_map/ppermute | solution.py:15
  185.8 5.2 %pad_maximum_fusion = bf16[1280,2,2,128]{3,2,0,1:T(2,128)(2,1)} fusion(bf16[1024,2,2,128]{3,2,0,1:T(2,128)(2,1)S(1)} %slice-done, bf16[256,2,2,128]{3,2,0,1:T(2,128)(2,1)S(1)} %collective-permute-done), kind=kLoop, calls=%fused_computation.58 | loop fusion | flops 655360 | bytes 2621440 | tf_op jit(solution)/shard_map/concatenate | solution.py:194
  191.1 31.2 %while.12 = (s32[]{:T(128)}, bf16[2,512,2,128]{3,2,1,0:T(2,128)(2,1)}, s32[2]{0:T(128)S(1)}, bf16[1280,2,2,128]{3,2,0,1:T(2,128)(2,1)}, s32[]{:T(128)}, /*index=...) while((s32[]{:T(128)}, ...), condition=%wide.region_9.10_spmd, body=%wide.region_6.9_spmd.sunk | while | flops 617092352 | bytes 11036708 | solution.py:70
  192.2 1.7 constant_dynamic-slice_fusion.5
  196.8 3.0 %fusion.107 = f32[2,512]{1,0:T(2,128)S(1)} fusion(s32[512,768]{1,0:T(8,128)} %broadcast_subtract_fusion.2, s32[2]{0:T(128)S(1)} %get-tuple-element.220, pred[768]{0:T(1024)(128)(4,1)S(1)} %broadcast_compare_fusion.4, pred[512,768]{1,0:T(8,128)(4,1)S(1)} %broadcast_compare_fusion.5, bf16[768,1,2,128]{3,2,0,1:T(2,128)(2,1)S(1)} %get-tuple-element.185, ...), kind=kOutput, calls=%fused_computation.146.clone.1 | convolution fusion | flops 206832384 | bytes 2626312 | tf_op jit(solution)/shard_map/while/body/eval_jaxpr/sub | solution.py:37
  199.8 4.9 %fusion.108 = bf16[1,512,2,128]{1,3,2,0:T(8,128)(2,1)} fusion(f32[2,512]{1,0:T(2,128)S(1)} %fusion.107, bf16[768,1,2,128]{3,2,0,1:T(2,128)(2,1)S(1)} %get-tuple-element.186, s32[512,768]{1,0:T(8,128)} %broadcast_subtract_fusion.2, s32[2]{0:T(128)S(1)} %get-tuple-element.220, pred[768]{0:T(1024)(128)(4,1)S(1)} %broadcast_compare_fusion.4, ...), kind=kOutput, calls=%fused_computation.13.clone.1 | convolution fusion | flops 409077504 | bytes 3281672 | tf_op jit(solution)/shard_map/while/body/eval_jaxpr/hqk,khd->qhd/dot_general | solution.py:40
  207.8 1.7 constant_dynamic-slice_fusion.5
  212.3 3.0 %fusion.107 = f32[2,512]{1,0:T(2,128)S(1)} fusion(s32[512,768]{1,0:T(8,128)} %broadcast_subtract_fusion.2, s32[2]{0:T(128)S(1)} %get-tuple-element.220, pred[768]{0:T(1024)(128)(4,1)S(1)} %broadcast_compare_fusion.4, pred[512,768]{1,0:T(8,128)(4,1)S(1)} %broadcast_compare_fusion.5, bf16[768,1,2,128]{3,2,0,1:T(2,128)(2,1)S(1)} %get-tuple-element.185, ...), kind=kOutput, calls=%fused_computation.146.clone.1 | convolution fusion | flops 206832384 | bytes 2626312 | tf_op jit(solution)/shard_map/while/body/eval_jaxpr/sub | solution.py:37
  215.4 4.9 %fusion.108 = bf16[1,512,2,128]{1,3,2,0:T(8,128)(2,1)} fusion(f32[2,512]{1,0:T(2,128)S(1)} %fusion.107, bf16[768,1,2,128]{3,2,0,1:T(2,128)(2,1)S(1)} %get-tuple-element.186, s32[512,768]{1,0:T(8,128)} %broadcast_subtract_fusion.2, s32[2]{0:T(128)S(1)} %get-tuple-element.220, pred[768]{0:T(1024)(128)(4,1)S(1)} %broadcast_compare_fusion.4, ...), kind=kOutput, calls=%fused_computation.13.clone.1 | convolution fusion | flops 409077504 | bytes 3281672 | tf_op jit(solution)/shard_map/while/body/eval_jaxpr/hqk,khd->qhd/dot_general | solution.py:40
  222.3 1.9 copy.207
  (101 shorter events, 31.6 us)
Async XLA Ops:
  7.2 124.9 %copy-start = (bf16[1024,1024]{1,0:T(8,128)(2,1)S(1)}, bf16[1024,1024]{1,0:T(8,128)(2,1)}, u32[]{:S(2)}) copy-start(bf16[1024,1024]{1,0:T(8,128)(2,1)} %param.21) | copy-start | bytes 6291460
  7.2 92.4 %all-gather.2.cloned.1.call-start = ((), (), s32[]{:S(2)}) async-start(), calls=%async_computation.2 | async-start | bytes 8519680 | tf_op jit(solution)/shard_map/all_gather | solution.py:104
  8.5 5.6 %copy-start.2 = (bf16[1024,256]{1,0:T(8,128)(2,1)S(1)}, bf16[1024,256]{1,0:T(8,128)(2,1)}, u32[]{:S(2)}) copy-start(bf16[1024,256]{1,0:T(8,128)(2,1)} %param.14) | copy-start | bytes 1572868
  14.2 3.7 %copy-start.11 = (f32[16,2,11]{0,1,2:T(2,128)S(1)}, f32[16,2,11]{0,1,2:T(2,128)}, u32[]{:S(2)}) copy-start(f32[16,2,11]{0,1,2:T(2,128)} %param.18) | copy-start | bytes 4228
  14.2 3.9 %copy-start.14 = (s32[1024]{0:T(1024)S(1)}, s32[1024]{0:T(1024)}, u32[]{:S(2)}) copy-start(s32[1024]{0:T(1024)} %param.17) | copy-start | bytes 12292
  19.6 3.2 %copy-start.1 = (f32[16,2,128,128]{3,2,1,0:T(8,128)S(1)}, f32[16,2,128,128]{3,2,1,0:T(8,128)}, u32[]{:S(2)}) copy-start(f32[16,2,128,128]{3,2,1,0:T(8,128)} %get-tuple-element.135) | copy-start | bytes 6291460
  22.8 1.0 copy-start.8
  25.4 1.0 copy-start.6
  27.8 4.4 %copy-start.7 = (bf16[2,512,2,128]{3,2,1,0:T(2,128)(2,1)S(1)}, bf16[2,512,2,128]{3,2,1,0:T(2,128)(2,1)}, u32[]{:S(2)}) copy-start(bf16[2,512,2,128]{3,2,1,0:T(2,128)(2,1)} %reshape_reshape.17) | copy-start | bytes 1572868
  36.2 3.3 %copy-start.5 = (bf16[16,64,2,128]{3,2,1,0:T(2,128)(2,1)S(1)}, bf16[16,64,2,128]{3,2,1,0:T(2,128)(2,1)}, u32[]{:S(2)}) copy-start(bf16[16,64,2,128]{3,2,1,0:T(2,128)(2,1)} %reshape.270) | copy-start | bytes 1572868
  44.1 1.5 copy-start.13
  99.5 10.7 %copy-start.9 = (bf16[1024,2,128]{2,1,0:T(2,128)(2,1)S(1)}, bf16[1024,2,128]{2,1,0:T(2,128)(2,1)}, u32[]{:S(2)}) copy-start(bf16[1024,2,128]{2,1,0:T(2,128)(2,1)} %reshape.278) | copy-start | bytes 1572868
  112.2 4.3 %copy-start.12 = (f32[256]{0:T(256)S(1)}, f32[256]{0:T(256)}, u32[]{:S(2)}) copy-start(f32[256]{0:T(256)} %param.19) | copy-start | bytes 3076
  114.8 1.7 copy-start.3
  132.0 2.7 %copy-start.15 = (f32[1024]{0:T(1024)S(1)}, f32[1024]{0:T(1024)}, u32[]{:S(2)}) copy-start(f32[1024]{0:T(1024)} %param.22) | copy-start | bytes 12292
  133.9 0.8 copy-start.10
  170.4 7.6 %copy-start.16 = (s32[8]{0:T(128)S(1)}, s32[8]{0:T(128)}, u32[]{:S(2)}) copy-start(s32[8]{0:T(128)} %param.24) | copy-start | bytes 100
  173.9 11.9 %slice-start = ((bf16[1024,3,2,128]{3,2,0,1:T(2,128)(2,1)}), bf16[1024,2,2,128]{3,2,0,1:T(2,128)(2,1)S(1)}, s32[]{:S(2)}) async-start(bf16[1024,3,2,128]{3,2,0,1:T(2,128)(2,1)} %reshape.282), calls=%async_computation.3 | async-start | bytes 2097152 | tf_op jit(solution)/shard_map/slice | solution.py:194
  175.8 10.0 %collective-permute-start = (bf16[256,2,2,128]{3,2,0,1:T(2,128)(2,1)}, bf16[256,2,2,128]{3,2,0,1:T(2,128)(2,1)S(1)}, u32[]{:S(2)}, u32[]{:S(2)}) collective-permute-start(bf16[256,2,2,128]{3,2,0,1:T(2,128)(2,1)} %slice.76), channel_id=1, source_target_pairs={{0,4},{4,8},{8,12},{12,16},{16,20},{20,24},{24,28},{28,32},{32,36}... | collective-permute-start | bytes 786440 | tf_op jit(solution)/shard_map/ppermute | solution.py:15
  178.0 1.4 copy-start.4
Sparse Core Ops, SparseCore 0:
  14.3 85.1 all-gather.1
where the time goes:
time: 232 us; the launch traced here: 231 us
  waiting for transfers between devices  59.2 us (26%)
  local copies, waits for them, and re-layouts  53.3 us (23%)
  matrix products  51.2 us (22%)
  blocking collectives  36.7 us (16%)
  between operations  14.4 us (6%)
  other arithmetic  12.9 us (6%)
    all_gather x1, waiting for transfers between devices, per_device(): piece = lax.all_gather(device_state[None], 'ctx', axis=0, tiled=True)  53.9 us
    all_to_all x1, blocking collectives, per_device(): lax.all_to_all(split_qkv, 'head', split_axis=2, concat_axis=0, tiled=True)  22.7 us
    all_to_all x1, blocking collectives, per_device(): lax.all_to_all(sectioned, 'head', split_axis=0, concat_axis=2, tiled=True)  14 us
    dot_general x1, matrix products, per_device(): remote = jnp.einsum('nb,nxy->bxy', member, piece, precision=PRECISE)  10.7 us
    dot_general x2, matrix products, attend_block(): jnp.einsum('hqk,khd->qhd', probs, value_block, preferred_element_type=jnp...  9.71 us
    transpose x3, local copies, waits for them, and re-layouts, per_device(): jnp.einsum('mthd,mhde->mthe', blocked_query, read_state, preferred_elemen...  6.39 us
    dot_general x4, matrix products, per_device(): jnp.einsum('mthd,mhde->mthe', blocked_query, read_state, preferred_elemen...  6.39 us
    sub x2, matrix products, attend_block(): weights = jnp.exp(scores - row_max)  6.09 us
  transfers between devices with their start and end apart: 2, of which 2 were waited for; matrix products, arithmetic and copies ran while one was open for 13% of the time, Pallas kernels for 0%

commit v1 on v0

--- a/solution.py
+++ b/solution.py
@@ -101,7 +101,9 @@
         "jchd,jche->jhde", key_stretches, value_stretches, preferred_element_type=jnp.float32
     )
     device_state = jnp.sum(states, 0).reshape(local_heads * head_dim, head_dim)
-    piece = lax.all_gather(device_state[None], "ctx", axis=0, tiled=True)
+    piece = jnp.concatenate(
+        lax.all_to_all(jnp.stack([device_state[None]] * lax.axis_size("ctx")), "ctx", 0, 0), axis=0
+    )
     piece_rows = piece.shape[0]
     source = jnp.arange(piece_rows, dtype=jnp.int32)
     span_sizes = 2 ** jnp.arange(ctx_bits, dtype=jnp.int32)

time: 232 us -> 324 us (1.40)
  waiting for transfers between devices: 59.2 us -> 160 us
  between operations: 14.4 us -> 1.06 us
  starting transfers between devices: 2.17 us -> 14 us
  matrix products: 51.2 us -> 41.1 us
  local copies, waits for them, and re-layouts: 53.3 us -> 60 us
    all_to_all x0 -> x1, waiting for transfers between devices: none -> 155 us  [per_device(): lax.all_to_all(jnp.stack([device_state[None]] * lax.axis_size('ctx')), 'c...]
    all_gather x1 -> x0, waiting for transfers between devices: 53.9 us -> none  [per_device(): piece = lax.all_gather(device_state[None], 'ctx', axis=0, tiled=True)]
    all_to_all x0 -> x1, starting transfers between devices: none -> 12.1 us  [per_device(): lax.all_to_all(jnp.stack([device_state[None]] * lax.axis_size('ctx')), 'c...]
    dot_general x0 -> x1, local copies, waits for them, and re-layouts: none -> 8.24 us  [per_device(): remote = jnp.einsum('nb,nxy->bxy', member, piece, precision=PRECISE)]
    dot_general x1, matrix products: 10.7 us -> 3.14 us  [per_device(): remote = jnp.einsum('nb,nxy->bxy', member, piece, precision=PRECISE)]
    another operation x0 -> x1, local copies, waits for them, and re-layouts: none -> 4.22 us  [per_device(): jnp.stack([device_state[None]] * lax.axis_size('ctx'))]
  transfers between devices with their start and end apart: 2 -> 2, of which waited for: 2 -> 2; matrix products, arithmetic and copies ran while one was open for 13% -> 10% of each run, Pallas kernels for 0% -> 0%
where the time goes in v1:
time: 324 us; the launch traced here: 323 us
  waiting for transfers between devices  160 us (49%)
  local copies, waits for them, and re-layouts  60 us (19%)
  matrix products  41.1 us (13%)
  blocking collectives  35.6 us (11%)
  starting transfers between devices  14 us (4%)
  other arithmetic  9.75 us (3%)
    all_to_all x1, waiting for transfers between devices, per_device(): lax.all_to_all(jnp.stack([device_state[None]] * lax.axis_size('ctx')), 'c...  155 us
    all_to_all x1, blocking collectives, per_device(): lax.all_to_all(split_qkv, 'head', split_axis=2, concat_axis=0, tiled=True)  22.1 us
    all_to_all x1, blocking collectives, per_device(): lax.all_to_all(sectioned, 'head', split_axis=0, concat_axis=2, tiled=True)  13.5 us
    all_to_all x1, starting transfers between devices, per_device(): lax.all_to_all(jnp.stack([device_state[None]] * lax.axis_size('ctx')), 'c...  12.1 us
    dot_general x2, matrix products, attend_block(): jnp.einsum('hqk,khd->qhd', probs, value_block, preferred_element_type=jnp...  9.26 us
    dot_general x1, local copies, waits for them, and re-layouts, per_device(): remote = jnp.einsum('nb,nxy->bxy', member, piece, precision=PRECISE)  8.24 us
    dot_general x4, matrix products, per_device(): jnp.einsum('mthd,mhde->mthe', blocked_query, read_state, preferred_elemen...  6.53 us
  transfers between devices with their start and end apart: 2, of which 2 were waited for; matrix products, arithmetic and copies ran while one was open for 10% of the time, Pallas kernels for 0%

profile of v1, /device:TPU:32, one launch (start us, length us, event | category | flops | bytes accessed | tf_op | source)
XLA Modules:
  0.0 323.2 jit_solution(17230935746629678055)
XLA Ops:
  3.1 1.9 fusion.91
  5.0 4.2 %stack.3 = f32[64,1,256,128]{3,2,1,0:T(8,128)} broadcast(f32[256,128]{1,0:T(8,128)S(1)} %bitcast.130), dimensions={2,3} | broadcast | bytes 8519680 | tf_op jit(solution)/shard_map/stack | solution.py:105
  9.2 12.1 %all-to-all-start = ((f32[64,1,256,128]{3,2,1,0:T(8,128)}), f32[64,1,256,128]{3,2,1,0:T(8,128)}, u32[]{:S(2)}, u32[]{:S(2)}) async-start(f32[64,1,256,128]{3,2,1,0:T(8,128)} %stack.3), calls=%async_computation | async-start | bytes 16777216 | tf_op jit(solution)/shard_map/all_to_all | solution.py:105
  26.7 3.2 slice.68
  34.9 2.6 copy.101
  37.5 1.7 bitcast_reduce_fusion
  40.7 2.6 copy.106
  43.3 3.3 %fusion.34 = f32[16,64,2,128]{3,1,2,0:T(8,128)} fusion(f32[15,2,128,128]{3,2,1,0:T(8,128)} %slice.68, f32[16]{0:T(128)S(1)} %fusion.79, f32[16,64,2]{1,2,0:T(2,128)S(1)} %copy.90, bf16[16,64,2,128]{3,2,1,0:T(2,128)(2,1)} %reshape.275), kind=kOutput, calls=%fused_computation.52 | convolution fusion | flops 68419584 | bytes 3547200 | tf_op jit(solution)/shard_map/mthd,mhde->mthe/dot_general | solution.py:147
  46.6 4.7 %fusion.33 = f32[16,64,2,128]{3,1,2,0:T(8,128)} fusion(f32[16,64,2,128]{3,1,2,0:T(8,128)} %fusion.34, f32[16,64,2,128]{3,1,0,2:T(8,128)} %bitcast.127, f32[16,64,2,128]{3,1,0,2:T(8,128)} %bitcast.126, f32[16,64,2,128]{3,1,0,2:T(8,128)} %bitcast.125, f32[16,64,2]{1,2,0:T(2,128)S(1)} %copy.103, f32[16,64,2]{1,2,0:T(2,128)S(1)} %copy.98, ...), kind=kOutput, calls=%fused_computation.50 | convolution fusion | flops 69468160 | bytes 6852608 | tf_op jit(solution)/shard_map/jhts,jshd->jthd/dot_general | solution.py:131
  52.8 154.5 %all-to-all-done = f32[64,1,256,128]{3,2,1,0:T(8,128)} async-done(((f32[64,1,256,128]{3,2,1,0:T(8,128)}), f32[64,1,256,128]{3,2,1,0:T(8,128)}, u32[]{:S(2)}, u32[]{:S(2)}) %all-to-all-start) | async-done | bytes 8388640 | tf_op jit(solution)/shard_map/all_to_all | solution.py:105
  207.3 8.2 %copy.109 = f32[256,128,64]{1,2,0:T(8,128)S(1)} copy(f32[256,128,64]{1,0,2:T(8,128)} %bitcast.27) | data formatting | bytes 16777216 | tf_op jit(solution)/shard_map/nb,nxy->bxy/dot_general | solution.py:115
  215.6 3.1 convolution_convert_fusion.1
  218.7 2.0 fusion.28
  220.8 2.6 copy.130
  223.4 1.7 multiply_reduce_fusion
  226.4 13.5 %all_to_all.35 = bf16[4,256,256]{2,1,0:T(8,128)(2,1)S(1)} all-to-all(bf16[4,256,256]{2,1,0:T(8,128)(2,1)S(1)} %reshape.287), channel_id=1, replica_groups=mesh['ctx'=64,'head'=4] {'head'}, dimensions={0} | all-to-all | bytes 1048576 | tf_op jit(solution)/shard_map/all_to_all | solution.py:178
  240.2 1.9 fusion.37
  242.9 5.8 %convolution_convert_fusion = bf16[256,3072]{1,0:T(8,128)(2,1)} fusion(bf16[1024,3072]{1,0:T(8,128)(2,1)} %param.23, bf16[256,1024]{1,0:T(8,128)(2,1)S(1)} %get-tuple-element.137, f32[1024]{0:T(1024)S(1)} %copy-done.16, f32[256]{0:T(256)S(1)} %add_rsqrt_fusion.1), kind=kOutput, calls=%fused_computation.36 | convolution fusion | flops 1612447744 | bytes 8393728 | tf_op jit(solution)/shard_map/dot_general | solution.py:187
  248.7 3.2 reshape.289
  252.2 22.1 %all_to_all.36 = bf16[256,3,4,256]{3,0,1,2:T(8,128)(2,1)S(1)} all-to-all(bf16[256,3,4,256]{3,0,1,2:T(8,128)(2,1)S(1)} %copy.114), channel_id=1, replica_groups=mesh['ctx'=64,'head'=4] {'head'}, dimensions={2} | all-to-all | bytes 3145728 | tf_op jit(solution)/shard_map/all_to_all | solution.py:190
  275.5 2.4 reshape.290
  278.1 1.9 collective-permute-start
  282.0 5.9 %collective-permute-done = bf16[256,2,2,128]{3,2,0,1:T(2,128)(2,1)S(1)} collective-permute-done((bf16[256,2,2,128]{3,2,0,1:T(2,128)(2,1)S(1)}, bf16[256,2,2,128]{3,2,0,1:T(2,128)(2,1)S(1)}, u32[]{:S(2)}, u32[]{:S(2)}) %collective-permute-start) | collective-permute-done | bytes 262176 | tf_op jit(solution)/shard_map/ppermute | solution.py:15
  287.9 4.4 %pad_maximum_fusion = bf16[1280,2,2,128]{3,2,0,1:T(2,128)(2,1)S(1)} fusion(bf16[1024,2,2,128]{3,2,0,1:T(2,128)(2,1)S(1)} %slice.77, bf16[256,2,2,128]{3,2,0,1:T(2,128)(2,1)S(1)} %collective-permute-done), kind=kLoop, calls=%fused_computation.56 | loop fusion | flops 655360 | bytes 2621440 | tf_op jit(solution)/shard_map/concatenate | solution.py:196
  292.3 28.8 %while.12 = (s32[]{:T(128)}, bf16[2,512,2,128]{3,2,1,0:T(2,128)(2,1)}, s32[2]{0:T(128)S(1)}, bf16[1280,2,2,128]{3,2,0,1:T(2,128)(2,1)S(1)}, s32[]{:T(128)}, /*in...) while((s32[]{:T(128)}, ...), condition=%wide.region_9.10_spmd, body=%wide.region_6.9_spmd.sunk | while | flops 617092352 | bytes 11036708 | solution.py:70
  295.0 1.8 constant_dynamic-slice_fusion.6
  297.4 2.7 fusion.103
  300.1 4.6 %fusion.104 = bf16[1,512,2,128]{1,3,2,0:T(8,128)(2,1)} fusion(f32[2,512]{1,0:T(2,128)S(1)} %fusion.103, bf16[768,1,2,128]{3,2,0,1:T(2,128)(2,1)} %get-tuple-element.186, s32[512,768]{1,0:T(8,128)S(1)} %broadcast_subtract_fusion.2, s32[2]{0:T(128)S(1)} %get-tuple-element.220, pred[768]{0:T(1024)(128)(4,1)S(1)} %broadcast_compare_fusion.4, ...), kind=kOutput, calls=%fused_computation.13.clone.1 | convolution fusion | flops 409077504 | bytes 3281672 | tf_op jit(solution)/shard_map/while/body/eval_jaxpr/hqk,khd->qhd/dot_general | solution.py:40
  309.4 1.8 constant_dynamic-slice_fusion.6
  311.8 2.7 fusion.103
  314.5 4.6 %fusion.104 = bf16[1,512,2,128]{1,3,2,0:T(8,128)(2,1)} fusion(f32[2,512]{1,0:T(2,128)S(1)} %fusion.103, bf16[768,1,2,128]{3,2,0,1:T(2,128)(2,1)} %get-tuple-element.186, s32[512,768]{1,0:T(8,128)S(1)} %broadcast_subtract_fusion.2, s32[2]{0:T(128)S(1)} %get-tuple-element.220, pred[768]{0:T(1024)(128)(4,1)S(1)} %broadcast_compare_fusion.4, ...), kind=kOutput, calls=%fused_computation.13.clone.1 | convolution fusion | flops 409077504 | bytes 3281672 | tf_op jit(solution)/shard_map/while/body/eval_jaxpr/hqk,khd->qhd/dot_general | solution.py:40
  321.2 2.1 copy.204
  (103 shorter events, 30.8 us)
Async XLA Ops:
  0.6 239.5 %copy-start = (bf16[1024,1024]{1,0:T(8,128)(2,1)S(1)}, bf16[1024,1024]{1,0:T(8,128)(2,1)}, u32[]{:S(2)}) copy-start(bf16[1024,1024]{1,0:T(8,128)(2,1)} %param.21) | copy-start | bytes 6291460
  3.1 1.9 copy-start.5
  9.2 12.1 %copy-start.3 = (bf16[1024,256]{1,0:T(8,128)(2,1)S(1)}, bf16[1024,256]{1,0:T(8,128)(2,1)}, u32[]{:S(2)}) copy-start(bf16[1024,256]{1,0:T(8,128)(2,1)} %param.14) | copy-start | bytes 1572868
  9.2 198.1 %all-to-all-start = ((f32[64,1,256,128]{3,2,1,0:T(8,128)}), f32[64,1,256,128]{3,2,1,0:T(8,128)}, u32[]{:S(2)}, u32[]{:S(2)}) async-start(f32[64,1,256,128]{3,2,1,0:T(8,128)} %stack.3), calls=%async_computation | async-start | bytes 16777216 | tf_op jit(solution)/shard_map/all_to_all | solution.py:105
  21.3 3.7 %copy-start.12 = (f32[16,2,11]{0,1,2:T(2,128)S(1)}, f32[16,2,11]{0,1,2:T(2,128)}, u32[]{:S(2)}) copy-start(f32[16,2,11]{0,1,2:T(2,128)} %param.18) | copy-start | bytes 4228
  21.3 3.8 %copy-start.15 = (s32[1024]{0:T(1024)S(1)}, s32[1024]{0:T(1024)}, u32[]{:S(2)}) copy-start(s32[1024]{0:T(1024)} %param.17) | copy-start | bytes 12292
  26.7 3.2 copy-start.2
  29.9 1.0 copy-start.9
  32.4 1.0 copy-start.7
  34.9 4.4 %copy-start.8 = (bf16[2,512,2,128]{3,2,1,0:T(2,128)(2,1)S(1)}, bf16[2,512,2,128]{3,2,1,0:T(2,128)(2,1)}, u32[]{:S(2)}) copy-start(bf16[2,512,2,128]{3,2,1,0:T(2,128)(2,1)} %reshape_reshape.17) | copy-start | bytes 1572868
  43.2 3.4 %copy-start.6 = (bf16[16,64,2,128]{3,2,1,0:T(2,128)(2,1)S(1)}, bf16[16,64,2,128]{3,2,1,0:T(2,128)(2,1)}, u32[]{:S(2)}) copy-start(bf16[16,64,2,128]{3,2,1,0:T(2,128)(2,1)} %copy-done.5) | copy-start | bytes 1572868
  51.3 1.5 copy-start.14
  215.6 3.2 copy-start.10
  220.8 4.3 %copy-start.13 = (f32[256]{0:T(256)S(1)}, f32[256]{0:T(256)}, u32[]{:S(2)}) copy-start(f32[256]{0:T(256)} %param.19) | copy-start | bytes 3076
  223.4 1.7 copy-start.4
  240.1 2.7 copy-start.16
  242.1 0.8 copy-start.11
  275.5 4.5 %copy-start.17 = (s32[8]{0:T(128)S(1)}, s32[8]{0:T(128)}, u32[]{:S(2)}) copy-start(s32[8]{0:T(128)} %param.24) | copy-start | bytes 100
  278.1 9.8 %collective-permute-start = (bf16[256,2,2,128]{3,2,0,1:T(2,128)(2,1)S(1)}, bf16[256,2,2,128]{3,2,0,1:T(2,128)(2,1)S(1)}, u32[]{:S(2)}, u32[]{:S(2)}) collective-permute-start(bf16[256,2,2,128]{3,2,0,1:T(2,128)(2,1)S(1)} %slice.76), channel_id=1, source_target_pairs={{0,4},{4,8},{8,12},{12,16},{16,20},{20,24},{24,28},{28,32},{32,36}... | collective-permute-start | bytes 786440 | tf_op jit(solution)/shard_map/ppermute | solution.py:15
  321.2 2.1 copy-start.1
